TPU v7x, 32 devices: a whole 2x2x4 slice. The times are simulated.
32 devices in a mesh: group: 4 (over y, core), shard: 8 (over z, x).
Axes of the slice: x: 2, y: 2, z: 4, core: 2. Of those that a mesh axis runs over, the one named last changes fastest.
Arguments:
- queries: bfloat16 [512, 32, 128], P(('group', 'shard')), may hold values from -12 to 12
- passages: bfloat16 [2048, 64, 128], P(('group', 'shard')), may hold values from -4 to 4
- candidates: int32 [512, 160], P(('group', 'shard')), may hold values from 0 to 2047, as said below
- passage_slot: int32 [2048], replicated, may hold values from 0 to 2047, as said below
Outputs:
- scores: float32 [512, 160], P(('group', 'shard'))
Inputs may be any that keep to these rules, and one draw needn't show every extreme that they name: `passage_slot`: every storage row is named by exactly one passage id. `candidates`: candidates k * 20 to (k + 1) * 20 - 1 of a query, for k < 8, all lie in the storage rows of one device, rows d * 64 to (d + 1) * 64 - 1 of device d counted group-major. Over the 16 queries of one device, at most 12 such groups name any one device, and some devices are named exactly 12 times by the queries of every device.
All inputs are finite; a program needn't handle non-finite values.
Results may differ from a plain program's by a relative error of at most 0.0003.
Values may be sent and summed in bfloat16 or wider, within the bound.
No kernel may reach another device: no remote copies, remote signals or barrier semaphores. Data moves between devices by JAX's collectives and lax.ppermute only.
A program may use at most 64 MiB of HBM per device.

v0:
```python
import functools

import jax
import jax.numpy as jnp
from jax import lax
from jax.experimental import pallas as pl
from jax.experimental.pallas import tpu as pltpu
from jax.sharding import PartitionSpec as P

PER_VISIT = 20
LANES = 128
GROUP = 8
SETS = 4
AXES = ("group", "shard")


def lookup(tables, high, low):
    result = jnp.zeros(high.shape, tables[0].dtype)
    for row, table in enumerate(tables):
        picked = jnp.take_along_axis(table, low, axis=1, mode="promise_in_bounds")
        result = jnp.where(high == row, picked, result)
    return result


def prepare_kernel(shape, where_ref, query_ref, cand_ref, slot_ref, block_ref, pick_ref):
    shard_count, z_count, slot_dev, spread = shape
    query_count, qtok, dim = query_ref.shape
    cand_count = cand_ref.shape[1]
    width = pick_ref.shape[1]
    my_core = lax.rem(lax.div(where_ref[0], shard_count), 2)
    my_x = lax.rem(where_ref[0], 2)
    cand = cand_ref[...]
    cand = jnp.concatenate(
        [cand, jnp.zeros((query_count, width - cand_count), jnp.int32)], axis=1
    )
    tables = [
        jnp.broadcast_to(slot_ref[row : row + 1, :], (query_count, LANES))
        for row in range(slot_ref.shape[0])
    ]
    parts = []
    for part in range(width // LANES):
        ids = cand[:, part * LANES : (part + 1) * LANES]
        parts.append(lookup(tables, lax.div(ids, LANES), lax.rem(ids, LANES)))
    storage = jnp.concatenate(parts, axis=1)
    device = lax.div(storage, slot_dev)
    group = lax.div(device, shard_count)
    shard = lax.rem(device, shard_count)
    cell = lax.div(group, 2) * z_count + lax.div(shard, 2)
    code = (
        cell * SETS
        + jnp.bitwise_xor(lax.rem(group, 2), my_core) * 2
        + jnp.bitwise_xor(lax.rem(shard, 2), my_x)
    )
    pick_ref[...] = code * slot_dev + lax.rem(storage, slot_dev)
    lane = lax.broadcasted_iota(jnp.int32, (query_count, LANES), 1)
    named = jnp.zeros((query_count, LANES), jnp.float32)
    for visit in range(spread):
        first = visit * PER_VISIT
        hit = code[:, first : first + 1] == lane
        named = jnp.where(hit, 1.0, named)
    rows = query_count * qtok
    block_ref[0:rows, :] = query_ref[...].reshape(rows, dim)
    block_ref[rows : rows + query_count, :] = named.astype(jnp.bfloat16)


def prepare(where, queries, candidates, passage_slot, shape):
    query_count, qtok, dim = queries.shape
    width = -(-candidates.shape[1] // LANES) * LANES
    vmem = pl.BlockSpec(memory_space=pltpu.VMEM)
    return pl.pallas_call(
        functools.partial(prepare_kernel, shape),
        out_shape=(
            jax.ShapeDtypeStruct((query_count * (qtok + 1), dim), jnp.bfloat16),
            jax.ShapeDtypeStruct((query_count, width), jnp.int32),
        ),
        in_specs=[pl.BlockSpec(memory_space=pltpu.SMEM), vmem, vmem, vmem],
        out_specs=(vmem, vmem),
        name="prepare",
    )(where, queries, candidates, passage_slot.reshape(-1, LANES))


def score_kernel(plan, *refs):
    arrays_at, set_from, n_arrays, n_stores, has_carry, qtok, y_count, z_count = plan
    where_ref = refs[0]
    arrays = refs[1 : 1 + n_arrays]
    stores = refs[1 + n_arrays : 1 + n_arrays + n_stores]
    rest = refs[1 + n_arrays + n_stores :]
    if has_carry:
        rest = rest[1:]
    (out_ref, qs, ps, mask_v, mask_s, todo, setof, best, copy_sem) = rest
    slots, ptok, dim = stores[0].shape
    query_count = qs.shape[1] // (qtok + 1)
    rows = query_count * qtok
    source_count = len(arrays_at)
    my_y = lax.div(where_ref[0], 4 * z_count)
    my_z = lax.rem(lax.div(where_ref[0], 2), z_count)
    me = my_y * z_count + my_z

    q_copies = []
    for position, (array, index) in enumerate(arrays_at):
        source = arrays[array] if index is None else arrays[array].at[index]
        q_copies.append(pltpu.make_async_copy(source, qs.at[position], copy_sem.at[0]))
    p_copies = [
        pltpu.make_async_copy(store, ps.at[position], copy_sem.at[1])
        for position, store in enumerate(stores)
    ]
    for copy in q_copies:
        copy.start()
    for copy in p_copies:
        copy.start()
    for copy in q_copies:
        copy.wait()

    weight = lax.shift_left(1, lax.broadcasted_iota(jnp.int32, (query_count, LANES), 0))
    weight = weight.astype(jnp.float32)
    for position in range(source_count):
        named = qs[position, rows : rows + query_count, :].astype(jnp.float32)
        mask_v[position : position + 1, :] = jnp.sum(
            named * weight, axis=0, keepdims=True
        ).astype(jnp.int32)
    mask_copy = pltpu.make_async_copy(mask_v, mask_s, copy_sem.at[2])
    mask_copy.start()
    mask_copy.wait()

    total = jnp.int32(0)
    for position, (set_id, from_source) in enumerate(set_from):
        start = total

        def one_source(source, filled, set_id=set_id):
            bits = mask_s[source, me * SETS + set_id]
            for query in range(query_count):
                todo[filled] = source * query_count + query
                filled = filled + (lax.shift_right_logical(bits, query) & 1)
            return filled

        filled = lax.fori_loop(from_source, source_count, one_source, start)
        last = todo[jnp.maximum(filled - 1, 0)]
        for extra in range(GROUP - 1):
            todo[filled + extra] = last
        total = lax.div(filled + (GROUP - 1), GROUP) * GROUP

        def mark(group, carry, position=position):
            setof[group] = position
            return carry

        lax.fori_loop(lax.div(start, GROUP), lax.div(total, GROUP), mark, 0)
    groups = lax.div(total, GROUP)

    for copy in p_copies:
        copy.wait()

    columns = GROUP * qtok
    adder = jnp.where(
        lax.div(lax.broadcasted_iota(jnp.int32, (GROUP, columns), 1), qtok)
        == lax.broadcasted_iota(jnp.int32, (GROUP, columns), 0),
        1.0,
        0.0,
    ).astype(jnp.bfloat16)
    contract_last = (((1,), (1,)), ((), ()))
    quarter = lax.div(lax.broadcasted_iota(jnp.int32, (1, SETS * slots), 1), slots)

    def finish(group):
        value = best[...]
        high = value.astype(jnp.bfloat16)
        low = (value - high.astype(jnp.float32)).astype(jnp.bfloat16)
        score = lax.dot_general(adder, high, contract_last, preferred_element_type=jnp.float32)
        score += lax.dot_general(adder, low, contract_last, preferred_element_type=jnp.float32)
        score = score * (1.0 / qtok)
        score = jnp.concatenate([score] * SETS, axis=1)
        position = setof[group]
        set_id = jnp.int32(set_from[0][0])
        for other in range(1, len(set_from)):
            set_id = jnp.where(position == other, set_from[other][0], set_id)
        for item in range(GROUP):
            entry = todo[group * GROUP + item]
            source = lax.div(entry, query_count)
            from_y = lax.rem(my_y - lax.div(source, z_count) + y_count, y_count)
            from_z = lax.rem(my_z - lax.rem(source, z_count) + z_count, z_count)
            row = (from_y * z_count + from_z) * query_count + lax.rem(entry, query_count)
            out_ref[pl.ds(row, 1), :] = jnp.where(
                quarter == set_id, score[item : item + 1], out_ref[pl.ds(row, 1), :]
            )

    def search(group):
        pieces = []
        for item in range(GROUP):
            entry = todo[group * GROUP + item]
            source = lax.div(entry, query_count)
            first = pl.multiple_of(lax.rem(entry, query_count) * qtok, qtok)
            pieces.append(qs[source, pl.ds(first, qtok), :])
        query = jnp.concatenate(pieces, axis=0)
        position = setof[group]
        step = 8
        for first in range(0, slots, step):
            tokens = ps[position, first : first + step].reshape(step * ptok, dim)
            similarity = lax.dot_general(
                tokens, query, contract_last, preferred_element_type=jnp.float32
            )
            similarity = similarity.reshape(step, ptok // 8, 8, columns)
            top = similarity[:, 0]
            for other in range(1, ptok // 8):
                top = jnp.maximum(top, similarity[:, other])
            best[first : first + step, :] = jnp.max(top, axis=1)

    @pl.when(groups > 0)
    def _():
        search(0)

        @pl.loop(1, groups)
        def _(group):
            finish(group - 1)
            search(group)

        finish(groups - 1)


def score(where, arrays, arrays_at, stores, set_from, qtok, counts, carry):
    slots, ptok, dim = stores[0].shape
    block_rows = arrays[0].shape[-2]
    query_count = block_rows // (qtok + 1)
    source_count = len(arrays_at)
    cells = counts[0] * counts[1]
    mask_rows = -(-source_count // 8) * 8
    entries = len(set_from) * (source_count * query_count + GROUP) + 2 * GROUP
    plan = (
        tuple(arrays_at),
        tuple(set_from),
        len(arrays),
        len(stores),
        carry is not None,
        qtok,
        *counts,
    )
    operands = [where, *arrays, *stores]
    aliases = {}
    specs = [pl.BlockSpec(memory_space=pltpu.SMEM)]
    specs += [pl.BlockSpec(memory_space=pl.ANY)] * (len(arrays) + len(stores))
    if carry is not None:
        aliases = {len(operands): 0}
        operands.append(carry)
        specs.append(pl.BlockSpec(memory_space=pltpu.VMEM))
    work = sum(source_count - from_source for _, from_source in set_from) * query_count // 4
    return pl.pallas_call(
        functools.partial(score_kernel, plan),
        out_shape=jax.ShapeDtypeStruct((cells * query_count, SETS * slots), jnp.float32),
        in_specs=specs,
        out_specs=pl.BlockSpec(memory_space=pltpu.VMEM),
        scratch_shapes=[
            pltpu.VMEM((source_count, block_rows, dim), jnp.bfloat16),
            pltpu.VMEM((len(stores), slots, ptok, dim), jnp.bfloat16),
            pltpu.VMEM((mask_rows, LANES), jnp.int32),
            pltpu.SMEM((mask_rows, LANES), jnp.int32),
            pltpu.SMEM((entries,), jnp.int32),
            pltpu.SMEM((entries // GROUP + 1,), jnp.int32),
            pltpu.VMEM((slots, GROUP * qtok), jnp.float32),
            pltpu.SemaphoreType.DMA((3,)),
        ],
        input_output_aliases=aliases,
        compiler_params=pltpu.CompilerParams(vmem_limit_bytes=48 << 20),
        cost_estimate=pl.CostEstimate(
            flops=4 * work * slots * ptok * qtok * dim,
            bytes_accessed=source_count * block_rows * dim * 2
            + len(stores) * slots * ptok * dim * 2,
            transcendentals=0,
        ),
    )(*operands)


def select_kernel(scores_ref, pick_ref, out_ref):
    cells, _, wide = scores_ref.shape
    cand_count = out_ref.shape[1]
    tables = [
        scores_ref[cell, :, part * LANES : (part + 1) * LANES]
        for cell in range(cells)
        for part in range(wide // LANES)
    ]
    parts = []
    for part in range(pick_ref.shape[1] // LANES):
        pick = pick_ref[:, part * LANES : (part + 1) * LANES]
        parts.append(lookup(tables, lax.div(pick, LANES), lax.rem(pick, LANES)))
    out_ref[...] = jnp.concatenate(parts, axis=1)[:, :cand_count]


def select(scores, pick, cand_count):
    vmem = pl.BlockSpec(memory_space=pltpu.VMEM)
    return pl.pallas_call(
        select_kernel,
        out_shape=jax.ShapeDtypeStruct((pick.shape[0], cand_count), jnp.float32),
        in_specs=[vmem, vmem],
        out_specs=vmem,
        name="select",
    )(scores, pick)


def local(mesh_shape, queries, passages, candidates, passage_slot):
    group_count, shard_count = mesh_shape
    y_count, z_count = group_count // 2, shard_count // 2
    cells = y_count * z_count
    query_count, qtok, _ = queries.shape
    slots = passages.shape[0]
    spread = candidates.shape[1] // PER_VISIT

    def index(yh, c, zh, x):
        return (yh * 2 + c) * shard_count + zh * 2 + x

    every = [
        (yh, c, zh, x)
        for yh in range(y_count)
        for c in range(2)
        for zh in range(z_count)
        for x in range(2)
    ]

    def move(value, to):
        pairs = [(index(*device), index(*to(*device))) for device in every]
        return lax.ppermute(value, AXES, pairs)

    group = lax.axis_index("group")
    shard = lax.axis_index("shard")
    where = (group * shard_count + shard).reshape(1).astype(jnp.int32)

    store_x = move(passages, lambda yh, c, zh, x: (yh, c, zh, 1 - x))
    store_c = move(passages, lambda yh, c, zh, x: (yh, 1 - c, zh, x))
    block, pick = prepare(
        where, queries, candidates, passage_slot, (shard_count, z_count, slots, spread)
    )
    line = [block] + [
        move(block, lambda yh, c, zh, x, kz=kz: (yh, c, (zh + kz) % z_count, x))
        for kz in range(1, z_count)
    ]
    blocks = list(line)
    for ky in range(1, y_count):
        blocks += [
            move(part, lambda yh, c, zh, x, ky=ky: ((yh + ky) % y_count, c, zh, x))
            for part in line
        ]
    at = [(position, None) for position in range(cells)]
    counts = (y_count, z_count)
    own = score(
        where, line, at[:z_count], [passages, store_c], [(0, 0), (2, 0)], qtok, counts, None
    )
    store_x, own = lax.optimization_barrier((store_x, own))
    store_xc = move(store_x, lambda yh, c, zh, x: (yh, 1 - c, zh, x))
    everything = score(
        where,
        blocks,
        at,
        [passages, store_c, store_x, store_xc],
        [(0, z_count), (2, z_count), (1, 0), (3, 0)],
        qtok,
        counts,
        own,
    )
    returned = everything.reshape(cells, query_count, SETS * slots)
    members = [
        [index(yh, c, zh, x) for yh in range(y_count) for zh in range(z_count)]
        for c in range(2)
        for x in range(2)
    ]
    returned = lax.all_to_all(
        returned, AXES, 0, 0, tiled=True, axis_index_groups=members
    )
    return select(returned, pick, candidates.shape[1])


def solution(mesh):
    mesh_shape = (mesh.shape["group"], mesh.shape["shard"])
    return jax.shard_map(
        functools.partial(local, mesh_shape),
        mesh=mesh,
        in_specs=(
            P(AXES, None, None),
            P(AXES, None, None),
            P(AXES, None),
            P(),
        ),
        out_specs=P(AXES, None),
        check_vma=False,
    )
```

profile of v0, /device:TPU:0, one launch (start us, length us, event | category | flops | bytes accessed | tf_op | source)
XLA Modules:
  0.0 71.7 jit_solution(11172300142810240704)
XLA Ops:
  0.0 0.5 collective-permute-start.7
  0.5 2.5 %collective-permute-start.8 = (bf16[64,64,128]{2,1,0:T(8,128)(2,1)}, bf16[64,64,128]{2,1,0:T(8,128)(2,1)S(1)}, u32[]{:S(2)}, u32[]{:S(2)}) collective-permute-start(bf16[64,64,128]{2,1,0:T(8,128)(2,1)} %refs_9_.1), channel_id=1, source_target_pairs={{0,1},{1,0},{2,3},{3,2},{4,5},{5,4},{6,7},{7,6},{8,9},{9,8},{10,11... | collective-permute-start | bytes 3145736 | tf_op jit(solution)/shard_map/ppermute | solution.py:316
  3.0 1.8 %prepare.1 = (bf16[528,128]{1,0:T(8,128)(2,1)}, s32[16,256]{1,0:T(8,128)}) custom-call(s32[1]{0:T(128)} %bitcast.where_ref.refs_0_, bf16[16,32,128]{2,1,0:T(8,128)(2,1)} %query_ref.1, s32[16,160]{1,0:T(8,128)} %cand_ref.1, s32[16,128]{1,0:T(8,128)} %bitcast.4), custom_call_target="tpu_custom_call" | custom-call | tf_op jit(solution)/shard_map/prepare/pallas_call | solution.py:70
  4.8 3.6 %collective-permute-start.2 = (bf16[528,128]{1,0:T(8,128)(2,1)}, bf16[528,128]{1,0:T(8,128)(2,1)S(1)}, u32[]{:S(2)}, u32[]{:S(2)}) collective-permute-start(bf16[528,128]{1,0:T(8,128)(2,1)} %get-tuple-element.9.refs_1_), channel_id=1, source_target_pairs={{0,6},{1,7},{2,0},{3,1},{4,2},{5,3},{6,4},{7,5},{8,14},{9,15},{10,... | collective-permute-start | bytes 405512 | tf_op jit(solution)/shard_map/ppermute | solution.py:316
  8.4 0.0 collective-permute-start.1
  8.4 1.0 %collective-permute-start = (bf16[528,128]{1,0:T(8,128)(2,1)}, bf16[528,128]{1,0:T(8,128)(2,1)S(1)}, u32[]{:S(2)}, u32[]{:S(2)}) collective-permute-start(bf16[528,128]{1,0:T(8,128)(2,1)} %get-tuple-element.9.refs_1_), channel_id=1, source_target_pairs={{0,2},{1,3},{2,4},{3,5},{4,6},{5,7},{6,0},{7,1},{8,10},{9,11},{10,... | collective-permute-start | bytes 405512 | tf_op jit(solution)/shard_map/ppermute | solution.py:316
  9.4 3.4 %collective-permute-done.2.refs_4_ = bf16[528,128]{1,0:T(8,128)(2,1)S(1)} collective-permute-done((bf16[528,128]{1,0:T(8,128)(2,1)}, bf16[528,128]{1,0:T(8,128)(2,1)S(1)}, u32[]{:S(2)}, u32[]{:S(2)}) %collective-permute-start.2) | collective-permute-done | bytes 135200 | tf_op jit(solution)/shard_map/ppermute | solution.py:316
  12.8 7.9 %collective-permute-done.1.refs_3_ = bf16[528,128]{1,0:T(8,128)(2,1)S(1)} collective-permute-done((bf16[528,128]{1,0:T(8,128)(2,1)}, bf16[528,128]{1,0:T(8,128)(2,1)S(1)}, u32[]{:S(2)}, u32[]{:S(2)}) %collective-permute-start.1) | collective-permute-done | bytes 135200 | tf_op jit(solution)/shard_map/ppermute | solution.py:316
  20.7 0.0 collective-permute-done.refs_2_
  20.7 0.0 collective-permute-done.7.refs_6_.refs_10_
  20.7 0.0 copy-start
  20.7 1.2 %copy-done = bf16[64,64,128]{2,1,0:T(8,128)(2,1)S(1)} copy-done((bf16[64,64,128]{2,1,0:T(8,128)(2,1)S(1)}, bf16[64,64,128]{2,1,0:T(8,128)(2,1)}, u32[]{:S(2)}) %copy-start) | copy-done | bytes 1048600
  22.0 0.0 copy-start.1
  22.0 0.9 %copy-done.1 = bf16[528,128]{1,0:T(8,128)(2,1)S(1)} copy-done((bf16[528,128]{1,0:T(8,128)(2,1)S(1)}, bf16[528,128]{1,0:T(8,128)(2,1)}, u32[]{:S(2)}) %copy-start.1) | copy-done | bytes 135192
  22.9 7.2 %shard_map.46.refs_13_ = f32[128,256]{1,0:T(8,128)S(1)} custom-call(s32[1]{0:T(128)} %bitcast.where_ref.refs_0_, bf16[528,128]{1,0:T(8,128)(2,1)S(1)} %copy-done.1, bf16[528,128]{1,0:T(8,128)(2,1)S(1)} %collective-permute-done.refs_2_, bf16[528,128]{1,0:T(8,128)(2,1)S(1)} %collective-permute-done.1.refs_3_, ...), custom_call_target="tpu_custom_call" | custom-call | flops 2147483648 | bytes 2637824 | tf_op jit(solution)/shard_map/pallas_call | solution.py:243
  30.1 0.0 collective-permute-done.8.refs_11_
  30.1 0.1 collective-permute-start.9
  30.2 0.1 collective-permute-start.3
  30.3 2.0 %collective-permute-start.6 = (bf16[528,128]{1,0:T(8,128)(2,1)S(1)}, bf16[528,128]{1,0:T(8,128)(2,1)S(1)}, u32[]{:S(2)}, u32[]{:S(2)}) collective-permute-start(bf16[528,128]{1,0:T(8,128)(2,1)S(1)} %collective-permute-done.2.refs_4_), channel_id=1, source_target_pairs={{0,16},{1,17},{2,18},{3,19},{4,20},{5,21},{6,22},{7,23},{8,24},{9,... | collective-permute-start | bytes 405512 | tf_op jit(solution)/shard_map/ppermute | solution.py:316
  32.3 0.1 collective-permute-start.5
  32.3 1.9 %collective-permute-start.4 = (bf16[528,128]{1,0:T(8,128)(2,1)S(1)}, bf16[528,128]{1,0:T(8,128)(2,1)S(1)}, u32[]{:S(2)}, u32[]{:S(2)}) collective-permute-start(bf16[528,128]{1,0:T(8,128)(2,1)S(1)} %collective-permute-done.refs_2_), channel_id=1, source_target_pairs={{0,16},{1,17},{2,18},{3,19},{4,20},{5,21},{6,22},{7,23},{8,24},{9,... | collective-permute-start | bytes 405512 | tf_op jit(solution)/shard_map/ppermute | solution.py:316
  34.3 2.4 %collective-permute-done.3.refs_5_ = bf16[528,128]{1,0:T(8,128)(2,1)S(1)} collective-permute-done((bf16[528,128]{1,0:T(8,128)(2,1)S(1)}, bf16[528,128]{1,0:T(8,128)(2,1)S(1)}, u32[]{:S(2)}, u32[]{:S(2)}) %collective-permute-start.3) | collective-permute-done | bytes 135200 | tf_op jit(solution)/shard_map/ppermute | solution.py:316
  36.7 2.9 %collective-permute-done.6.refs_8_ = bf16[528,128]{1,0:T(8,128)(2,1)S(1)} collective-permute-done((bf16[528,128]{1,0:T(8,128)(2,1)S(1)}, bf16[528,128]{1,0:T(8,128)(2,1)S(1)}, u32[]{:S(2)}, u32[]{:S(2)}) %collective-permute-start.6) | collective-permute-done | bytes 135200 | tf_op jit(solution)/shard_map/ppermute | solution.py:316
  39.6 2.9 %collective-permute-done.5.refs_7_ = bf16[528,128]{1,0:T(8,128)(2,1)S(1)} collective-permute-done((bf16[528,128]{1,0:T(8,128)(2,1)S(1)}, bf16[528,128]{1,0:T(8,128)(2,1)S(1)}, u32[]{:S(2)}, u32[]{:S(2)}) %collective-permute-start.5) | collective-permute-done | bytes 135200 | tf_op jit(solution)/shard_map/ppermute | solution.py:316
  42.5 2.4 %collective-permute-done.4.refs_6_ = bf16[528,128]{1,0:T(8,128)(2,1)S(1)} collective-permute-done((bf16[528,128]{1,0:T(8,128)(2,1)S(1)}, bf16[528,128]{1,0:T(8,128)(2,1)S(1)}, u32[]{:S(2)}, u32[]{:S(2)}) %collective-permute-start.4) | collective-permute-done | bytes 135200 | tf_op jit(solution)/shard_map/ppermute | solution.py:316
  44.9 0.0 collective-permute-done.9.refs_12_
  44.9 12.3 %shard_map.47 = f32[128,256]{1,0:T(8,128)S(1)} custom-call(s32[1]{0:T(128)} %bitcast.where_ref.refs_0_, bf16[528,128]{1,0:T(8,128)(2,1)S(1)} %copy-done.1, bf16[528,128]{1,0:T(8,128)(2,1)S(1)} %collective-permute-done.refs_2_, bf16[528,128]{1,0:T(8,128)(2,1)S(1)} %collective-permute-done.1.refs_3_, ...), custom_call_target="tpu_custom_call", output_to_operand_aliasing={{}: (13, {})} | custom-call | flops 6442450944 | bytes 5275648 | tf_op jit(solution)/shard_map/pallas_call | solution.py:243
  57.1 12.9 %all_to_all.5.scores_ref = f32[8,16,256]{2,1,0:T(8,128)} all-to-all(f32[8,16,256]{2,1,0:T(8,128)S(1)} %bitcast.3), channel_id=1, replica_groups={{0,2,4,6,16,18,20,22},{1,3,5,7,17,19,21,23},{8,10,12,14,24,26,28,30},{9..., dimensions={0} | all-to-all | bytes 262144 | tf_op jit(solution)/shard_map/all_to_all | solution.py:360
  70.0 1.7 %select.1 = f32[16,160]{1,0:T(8,128)} custom-call(f32[8,16,256]{2,1,0:T(8,128)} %all_to_all.5.scores_ref, s32[16,256]{1,0:T(8,128)} %get-tuple-element.12.pick_ref), custom_call_target="tpu_custom_call" | custom-call | tf_op jit(solution)/shard_map/select/pallas_call | solution.py:286
Async XLA Ops:
  0.0 20.7 %collective-permute-start.7 = (bf16[64,64,128]{2,1,0:T(8,128)(2,1)}, bf16[64,64,128]{2,1,0:T(8,128)(2,1)S(1)}, u32[]{:S(2)}, u32[]{:S(2)}) collective-permute-start(bf16[64,64,128]{2,1,0:T(8,128)(2,1)} %refs_9_.1), channel_id=1, source_target_pairs={{0,8},{1,9},{2,10},{3,11},{4,12},{5,13},{6,14},{7,15},{8,0},{9,1},... | collective-permute-start | bytes 3145736 | tf_op jit(solution)/shard_map/ppermute | solution.py:316
  0.5 29.6 %collective-permute-start.8 = (bf16[64,64,128]{2,1,0:T(8,128)(2,1)}, bf16[64,64,128]{2,1,0:T(8,128)(2,1)S(1)}, u32[]{:S(2)}, u32[]{:S(2)}) collective-permute-start(bf16[64,64,128]{2,1,0:T(8,128)(2,1)} %refs_9_.1), channel_id=1, source_target_pairs={{0,1},{1,0},{2,3},{3,2},{4,5},{5,4},{6,7},{7,6},{8,9},{9,8},{10,11... | collective-permute-start | bytes 3145736 | tf_op jit(solution)/shard_map/ppermute | solution.py:316
  4.8 8.0 %collective-permute-start.2 = (bf16[528,128]{1,0:T(8,128)(2,1)}, bf16[528,128]{1,0:T(8,128)(2,1)S(1)}, u32[]{:S(2)}, u32[]{:S(2)}) collective-permute-start(bf16[528,128]{1,0:T(8,128)(2,1)} %get-tuple-element.9.refs_1_), channel_id=1, source_target_pairs={{0,6},{1,7},{2,0},{3,1},{4,2},{5,3},{6,4},{7,5},{8,14},{9,15},{10,... | collective-permute-start | bytes 405512 | tf_op jit(solution)/shard_map/ppermute | solution.py:316
  8.4 12.3 %collective-permute-start.1 = (bf16[528,128]{1,0:T(8,128)(2,1)}, bf16[528,128]{1,0:T(8,128)(2,1)S(1)}, u32[]{:S(2)}, u32[]{:S(2)}) collective-permute-start(bf16[528,128]{1,0:T(8,128)(2,1)} %get-tuple-element.9.refs_1_), channel_id=1, source_target_pairs={{0,4},{1,5},{2,6},{3,7},{4,0},{5,1},{6,2},{7,3},{8,12},{9,13},{10,... | collective-permute-start | bytes 405512 | tf_op jit(solution)/shard_map/ppermute | solution.py:316
  8.4 12.3 %collective-permute-start = (bf16[528,128]{1,0:T(8,128)(2,1)}, bf16[528,128]{1,0:T(8,128)(2,1)S(1)}, u32[]{:S(2)}, u32[]{:S(2)}) collective-permute-start(bf16[528,128]{1,0:T(8,128)(2,1)} %get-tuple-element.9.refs_1_), channel_id=1, source_target_pairs={{0,2},{1,3},{2,4},{3,5},{4,6},{5,7},{6,0},{7,1},{8,10},{9,11},{10,... | collective-permute-start | bytes 405512 | tf_op jit(solution)/shard_map/ppermute | solution.py:316
  20.7 1.2 %copy-start = (bf16[64,64,128]{2,1,0:T(8,128)(2,1)S(1)}, bf16[64,64,128]{2,1,0:T(8,128)(2,1)}, u32[]{:S(2)}) copy-start(bf16[64,64,128]{2,1,0:T(8,128)(2,1)} %refs_9_.1) | copy-start | bytes 3145732
  22.0 0.9 %copy-start.1 = (bf16[528,128]{1,0:T(8,128)(2,1)S(1)}, bf16[528,128]{1,0:T(8,128)(2,1)}, u32[]{:S(2)}) copy-start(bf16[528,128]{1,0:T(8,128)(2,1)} %get-tuple-element.9.refs_1_) | copy-start | bytes 405508
  30.1 14.8 %collective-permute-start.9 = (bf16[64,64,128]{2,1,0:T(8,128)(2,1)S(1)}, bf16[64,64,128]{2,1,0:T(8,128)(2,1)S(1)}, u32[]{:S(2)}, u32[]{:S(2)}) collective-permute-start(bf16[64,64,128]{2,1,0:T(8,128)(2,1)S(1)} %collective-permute-done.8.refs_11_), channel_id=1, source_target_pairs={{0,8},{1,9},{2,10},{3,11},{4,12},{5,13},{6,14},{7,15},{8,0},{9,1},... | collective-permute-start | bytes 3145736 | tf_op jit(solution)/shard_map/ppermute | solution.py:316
  30.2 6.5 %collective-permute-start.3 = (bf16[528,128]{1,0:T(8,128)(2,1)S(1)}, bf16[528,128]{1,0:T(8,128)(2,1)S(1)}, u32[]{:S(2)}, u32[]{:S(2)}) collective-permute-start(bf16[528,128]{1,0:T(8,128)(2,1)S(1)} %copy-done.1), channel_id=1, source_target_pairs={{0,16},{1,17},{2,18},{3,19},{4,20},{5,21},{6,22},{7,23},{8,24},{9,... | collective-permute-start | bytes 405512 | tf_op jit(solution)/shard_map/ppermute | solution.py:316
  30.3 9.3 %collective-permute-start.6 = (bf16[528,128]{1,0:T(8,128)(2,1)S(1)}, bf16[528,128]{1,0:T(8,128)(2,1)S(1)}, u32[]{:S(2)}, u32[]{:S(2)}) collective-permute-start(bf16[528,128]{1,0:T(8,128)(2,1)S(1)} %collective-permute-done.2.refs_4_), channel_id=1, source_target_pairs={{0,16},{1,17},{2,18},{3,19},{4,20},{5,21},{6,22},{7,23},{8,24},{9,... | collective-permute-start | bytes 405512 | tf_op jit(solution)/shard_map/ppermute | solution.py:316
  32.3 10.2 %collective-permute-start.5 = (bf16[528,128]{1,0:T(8,128)(2,1)S(1)}, bf16[528,128]{1,0:T(8,128)(2,1)S(1)}, u32[]{:S(2)}, u32[]{:S(2)}) collective-permute-start(bf16[528,128]{1,0:T(8,128)(2,1)S(1)} %collective-permute-done.1.refs_3_), channel_id=1, source_target_pairs={{0,16},{1,17},{2,18},{3,19},{4,20},{5,21},{6,22},{7,23},{8,24},{9,... | collective-permute-start | bytes 405512 | tf_op jit(solution)/shard_map/ppermute | solution.py:316
  32.3 12.5 %collective-permute-start.4 = (bf16[528,128]{1,0:T(8,128)(2,1)S(1)}, bf16[528,128]{1,0:T(8,128)(2,1)S(1)}, u32[]{:S(2)}, u32[]{:S(2)}) collective-permute-start(bf16[528,128]{1,0:T(8,128)(2,1)S(1)} %collective-permute-done.refs_2_), channel_id=1, source_target_pairs={{0,16},{1,17},{2,18},{3,19},{4,20},{5,21},{6,22},{7,23},{8,24},{9,... | collective-permute-start | bytes 405512 | tf_op jit(solution)/shard_map/ppermute | solution.py:316
where the time goes:
time: 72 us; the launch traced here: 71.7 us
  Pallas kernels  23 us (32%)
  waiting for transfers between devices  21.9 us (30%)
  blocking collectives  12.9 us (18%)
  starting transfers between devices  11.8 us (16%)
  local copies, waits for them, and re-layouts  2.13 us (3%)
    ppermute x10, waiting for transfers between devices, move(): return lax.ppermute(value, AXES, pairs)  21.9 us
    pallas_call x2, Pallas kernels, score(): pl.pallas_call(functools.partial(score_kernel, plan), out_shape=jax.Shape...  19.5 us
    all_to_all x1, blocking collectives, local(): lax.all_to_all(returned, AXES, 0, 0, tiled=True, axis_index_groups=members)  12.9 us
    ppermute x10, starting transfers between devices, move(): return lax.ppermute(value, AXES, pairs)  11.8 us
    unnamed x4, local copies, waits for them, and re-layouts  2.13 us
    pallas_call x1, Pallas kernels, prepare(): pl.pallas_call(functools.partial(prepare_kernel, shape), out_shape=(jax.S...  1.84 us
    pallas_call x1, Pallas kernels, select(): pl.pallas_call(select_kernel, out_shape=jax.ShapeDtypeStruct((pick.shape[...  1.69 us
  transfers between devices with their start and end apart: 10, of which 6 were waited for; matrix products, arithmetic and copies ran while one was open for 0% of the time, Pallas kernels for 13%

commit v1 on v0

--- a/solution.py
+++ b/solution.py
@@ -22,7 +22,11 @@
     return result
 
 
-def prepare_kernel(shape, where_ref, query_ref, cand_ref, slot_ref, block_ref, pick_ref):
+def prepare_kernel(
+    shape, where_ref, query_ref, cand_ref, slot_ref, store_ref, block_ref, pick_ref, near_ref, sem
+):
+    near_copy = pltpu.make_async_copy(store_ref, near_ref, sem)
+    near_copy.start()
     shard_count, z_count, slot_dev, spread = shape
     query_count, qtok, dim = query_ref.shape
     cand_count = cand_ref.shape[1]
@@ -61,9 +65,10 @@
     rows = query_count * qtok
     block_ref[0:rows, :] = query_ref[...].reshape(rows, dim)
     block_ref[rows : rows + query_count, :] = named.astype(jnp.bfloat16)
-
-
-def prepare(where, queries, candidates, passage_slot, shape):
+    near_copy.wait()
+
+
+def prepare(where, queries, candidates, passage_slot, passages, shape):
     query_count, qtok, dim = queries.shape
     width = -(-candidates.shape[1] // LANES) * LANES
     vmem = pl.BlockSpec(memory_space=pltpu.VMEM)
@@ -72,49 +77,62 @@
         out_shape=(
             jax.ShapeDtypeStruct((query_count * (qtok + 1), dim), jnp.bfloat16),
             jax.ShapeDtypeStruct((query_count, width), jnp.int32),
+            jax.ShapeDtypeStruct(passages.shape, passages.dtype),
         ),
-        in_specs=[pl.BlockSpec(memory_space=pltpu.SMEM), vmem, vmem, vmem],
-        out_specs=(vmem, vmem),
+        in_specs=[
+            pl.BlockSpec(memory_space=pltpu.SMEM),
+            vmem,
+            vmem,
+            vmem,
+            pl.BlockSpec(memory_space=pl.ANY),
+        ],
+        out_specs=(vmem, vmem, pl.BlockSpec(memory_space=pl.ANY)),
+        scratch_shapes=[pltpu.SemaphoreType.DMA(())],
+        compiler_params=pltpu.CompilerParams(vmem_limit_bytes=8 << 20),
         name="prepare",
-    )(where, queries, candidates, passage_slot.reshape(-1, LANES))
+    )(where, queries, candidates, passage_slot, passages)
 
 
 def score_kernel(plan, *refs):
-    arrays_at, set_from, n_arrays, n_stores, has_carry, qtok, y_count, z_count = plan
+    source_count, base, set_ids, has_carry, qtok, y_count, z_count = plan
     where_ref = refs[0]
-    arrays = refs[1 : 1 + n_arrays]
-    stores = refs[1 + n_arrays : 1 + n_arrays + n_stores]
-    rest = refs[1 + n_arrays + n_stores :]
+    arrays = refs[1 : 1 + source_count]
+    stores = refs[1 + source_count : 1 + source_count + len(set_ids)]
+    rest = refs[1 + source_count + len(set_ids) :]
     if has_carry:
+        rest[1][...] = rest[0][...]
         rest = rest[1:]
-    (out_ref, qs, ps, mask_v, mask_s, todo, setof, best, copy_sem) = rest
+    (out_ref, qs, ms, ps, mask_v, mask_s, todo, setof, best, copy_sem) = rest
     slots, ptok, dim = stores[0].shape
-    query_count = qs.shape[1] // (qtok + 1)
-    rows = query_count * qtok
-    source_count = len(arrays_at)
+    rows = qs.shape[1]
+    query_count = rows // qtok
     my_y = lax.div(where_ref[0], 4 * z_count)
     my_z = lax.rem(lax.div(where_ref[0], 2), z_count)
     me = my_y * z_count + my_z
 
-    q_copies = []
-    for position, (array, index) in enumerate(arrays_at):
-        source = arrays[array] if index is None else arrays[array].at[index]
-        q_copies.append(pltpu.make_async_copy(source, qs.at[position], copy_sem.at[0]))
+    m_copies = [
+        pltpu.make_async_copy(
+            array.at[pl.ds(rows, query_count)], ms.at[position], copy_sem.at[3]
+        )
+        for position, array in enumerate(arrays)
+    ]
+    q_copies = [
+        pltpu.make_async_copy(array.at[pl.ds(0, rows)], qs.at[position], copy_sem.at[0])
+        for position, array in enumerate(arrays)
+    ]
     p_copies = [
         pltpu.make_async_copy(store, ps.at[position], copy_sem.at[1])
         for position, store in enumerate(stores)
     ]
-    for copy in q_copies:
+    for copy in m_copies + q_copies + p_copies:
         copy.start()
-    for copy in p_copies:
-        copy.start()
-    for copy in q_copies:
+    for copy in m_copies:
         copy.wait()
 
     weight = lax.shift_left(1, lax.broadcasted_iota(jnp.int32, (query_count, LANES), 0))
     weight = weight.astype(jnp.float32)
     for position in range(source_count):
-        named = qs[position, rows : rows + query_count, :].astype(jnp.float32)
+        named = ms[position].astype(jnp.float32)
         mask_v[position : position + 1, :] = jnp.sum(
             named * weight, axis=0, keepdims=True
         ).astype(jnp.int32)
@@ -123,7 +141,7 @@
     mask_copy.wait()
 
     total = jnp.int32(0)
-    for position, (set_id, from_source) in enumerate(set_from):
+    for position, set_id in enumerate(set_ids):
         start = total
 
         def one_source(source, filled, set_id=set_id):
@@ -133,7 +151,7 @@
                 filled = filled + (lax.shift_right_logical(bits, query) & 1)
             return filled
 
-        filled = lax.fori_loop(from_source, source_count, one_source, start)
+        filled = lax.fori_loop(0, source_count, one_source, start)
         last = todo[jnp.maximum(filled - 1, 0)]
         for extra in range(GROUP - 1):
             todo[filled + extra] = last
@@ -146,7 +164,7 @@
         lax.fori_loop(lax.div(start, GROUP), lax.div(total, GROUP), mark, 0)
     groups = lax.div(total, GROUP)
 
-    for copy in p_copies:
+    for copy in q_copies + p_copies:
         copy.wait()
 
     columns = GROUP * qtok
@@ -159,8 +177,8 @@
     contract_last = (((1,), (1,)), ((), ()))
     quarter = lax.div(lax.broadcasted_iota(jnp.int32, (1, SETS * slots), 1), slots)
 
-    def finish(group):
-        value = best[...]
+    def finish(group, slot):
+        value = best[slot]
         high = value.astype(jnp.bfloat16)
         low = (value - high.astype(jnp.float32)).astype(jnp.bfloat16)
         score = lax.dot_general(adder, high, contract_last, preferred_element_type=jnp.float32)
@@ -168,20 +186,20 @@
         score = score * (1.0 / qtok)
         score = jnp.concatenate([score] * SETS, axis=1)
         position = setof[group]
-        set_id = jnp.int32(set_from[0][0])
-        for other in range(1, len(set_from)):
-            set_id = jnp.where(position == other, set_from[other][0], set_id)
+        set_id = jnp.int32(set_ids[0])
+        for other in range(1, len(set_ids)):
+            set_id = jnp.where(position == other, set_ids[other], set_id)
         for item in range(GROUP):
             entry = todo[group * GROUP + item]
-            source = lax.div(entry, query_count)
+            source = base + lax.div(entry, query_count)
             from_y = lax.rem(my_y - lax.div(source, z_count) + y_count, y_count)
-            from_z = lax.rem(my_z - lax.rem(source, z_count) + z_count, z_count)
+            from_z = jnp.bitwise_xor(my_z, lax.rem(source, z_count))
             row = (from_y * z_count + from_z) * query_count + lax.rem(entry, query_count)
             out_ref[pl.ds(row, 1), :] = jnp.where(
                 quarter == set_id, score[item : item + 1], out_ref[pl.ds(row, 1), :]
             )
 
-    def search(group):
+    def search(group, slot):
         pieces = []
         for item in range(GROUP):
             entry = todo[group * GROUP + item]
@@ -200,67 +218,82 @@
             top = similarity[:, 0]
             for other in range(1, ptok // 8):
                 top = jnp.maximum(top, similarity[:, other])
-            best[first : first + step, :] = jnp.max(top, axis=1)
-
-    @pl.when(groups > 0)
+            best[slot, first : first + step, :] = jnp.max(top, axis=1)
+
+    pairs = lax.div(groups, 2)
+    odd = groups > 2 * pairs
+
+    def search_pair(pair):
+        search(2 * pair, 0)
+        search(2 * pair + 1, 1)
+
+    def finish_pair(pair):
+        finish(2 * pair, 0)
+        finish(2 * pair + 1, 1)
+
+    @pl.when(pairs > 0)
     def _():
-        search(0)
-
-        @pl.loop(1, groups)
-        def _(group):
-            finish(group - 1)
-            search(group)
-
-        finish(groups - 1)
-
-
-def score(where, arrays, arrays_at, stores, set_from, qtok, counts, carry):
-    slots, ptok, dim = stores[0].shape
-    block_rows = arrays[0].shape[-2]
+        search_pair(0)
+
+        @pl.loop(1, pairs)
+        def _(pair):
+            finish_pair(pair - 1)
+            search_pair(pair)
+
+        @pl.when(odd)
+        def _():
+            finish_pair(pairs - 1)
+            search(groups - 1, 0)
+            finish(groups - 1, 0)
+
+        @pl.when(jnp.logical_not(odd))
+        def _():
+            finish_pair(pairs - 1)
+
+    @pl.when(groups == 1)
+    def _():
+        search(0, 0)
+        finish(0, 0)
+
+
+def score(where, arrays, base, stores, counts, qtok, carry):
+    set_ids = tuple(stores)
+    slots, ptok, dim = stores[set_ids[0]].shape
+    block_rows = arrays[0].shape[0]
     query_count = block_rows // (qtok + 1)
-    source_count = len(arrays_at)
+    source_count = len(arrays)
     cells = counts[0] * counts[1]
     mask_rows = -(-source_count // 8) * 8
-    entries = len(set_from) * (source_count * query_count + GROUP) + 2 * GROUP
-    plan = (
-        tuple(arrays_at),
-        tuple(set_from),
-        len(arrays),
-        len(stores),
-        carry is not None,
-        qtok,
-        *counts,
-    )
-    operands = [where, *arrays, *stores]
-    aliases = {}
+    entries = len(set_ids) * (source_count * query_count + GROUP) + 2 * GROUP
+    plan = (source_count, base, set_ids, carry is not None, qtok, *counts)
+    operands = [where, *arrays, *stores.values()]
     specs = [pl.BlockSpec(memory_space=pltpu.SMEM)]
-    specs += [pl.BlockSpec(memory_space=pl.ANY)] * (len(arrays) + len(stores))
+    specs += [pl.BlockSpec(memory_space=pl.ANY)] * (source_count + len(set_ids))
     if carry is not None:
-        aliases = {len(operands): 0}
         operands.append(carry)
         specs.append(pl.BlockSpec(memory_space=pltpu.VMEM))
-    work = sum(source_count - from_source for _, from_source in set_from) * query_count // 4
+    work = source_count * query_count * len(set_ids) // 4
     return pl.pallas_call(
         functools.partial(score_kernel, plan),
         out_shape=jax.ShapeDtypeStruct((cells * query_count, SETS * slots), jnp.float32),
         in_specs=specs,
         out_specs=pl.BlockSpec(memory_space=pltpu.VMEM),
         scratch_shapes=[
-            pltpu.VMEM((source_count, block_rows, dim), jnp.bfloat16),
-            pltpu.VMEM((len(stores), slots, ptok, dim), jnp.bfloat16),
+            pltpu.VMEM((source_count, query_count * qtok, dim), jnp.bfloat16),
+            pltpu.VMEM((source_count, query_count, dim), jnp.bfloat16),
+            pltpu.VMEM((len(set_ids), slots, ptok, dim), jnp.bfloat16),
             pltpu.VMEM((mask_rows, LANES), jnp.int32),
             pltpu.SMEM((mask_rows, LANES), jnp.int32),
             pltpu.SMEM((entries,), jnp.int32),
             pltpu.SMEM((entries // GROUP + 1,), jnp.int32),
-            pltpu.VMEM((slots, GROUP * qtok), jnp.float32),
-            pltpu.SemaphoreType.DMA((3,)),
+            pltpu.VMEM((2, slots, GROUP * qtok), jnp.float32),
+            pltpu.SemaphoreType.DMA((4,)),
         ],
-        input_output_aliases=aliases,
-        compiler_params=pltpu.CompilerParams(vmem_limit_bytes=48 << 20),
+        compiler_params=pltpu.CompilerParams(vmem_limit_bytes=24 << 20),
         cost_estimate=pl.CostEstimate(
             flops=4 * work * slots * ptok * qtok * dim,
             bytes_accessed=source_count * block_rows * dim * 2
-            + len(stores) * slots * ptok * dim * 2,
+            + len(set_ids) * slots * ptok * dim * 2,
             transcendentals=0,
         ),
     )(*operands)
@@ -288,6 +321,7 @@
         out_shape=jax.ShapeDtypeStruct((pick.shape[0], cand_count), jnp.float32),
         in_specs=[vmem, vmem],
         out_specs=vmem,
+        compiler_params=pltpu.CompilerParams(vmem_limit_bytes=8 << 20),
         name="select",
     )(scores, pick)
 
@@ -321,35 +355,30 @@
 
     store_x = move(passages, lambda yh, c, zh, x: (yh, c, zh, 1 - x))
     store_c = move(passages, lambda yh, c, zh, x: (yh, 1 - c, zh, x))
-    block, pick = prepare(
-        where, queries, candidates, passage_slot, (shard_count, z_count, slots, spread)
-    )
+    shape = (shard_count, z_count, slots, spread)
+    fixed = [
+        pltpu.with_memory_space_constraint(value, pltpu.HBM)
+        for value in (queries, candidates, passage_slot.reshape(-1, LANES), passages)
+    ]
+    block, pick, store = prepare(where, *fixed, shape)
     line = [block] + [
-        move(block, lambda yh, c, zh, x, kz=kz: (yh, c, (zh + kz) % z_count, x))
+        move(block, lambda yh, c, zh, x, kz=kz: (yh, c, zh ^ kz, x))
         for kz in range(1, z_count)
     ]
-    blocks = list(line)
-    for ky in range(1, y_count):
-        blocks += [
-            move(part, lambda yh, c, zh, x, ky=ky: ((yh + ky) % y_count, c, zh, x))
-            for part in line
-        ]
-    at = [(position, None) for position in range(cells)]
+    beside = [
+        move(part, lambda yh, c, zh, x, ky=ky: ((yh + ky) % y_count, c, zh, x))
+        for ky in range(1, y_count)
+        for part in line
+    ]
     counts = (y_count, z_count)
-    own = score(
-        where, line, at[:z_count], [passages, store_c], [(0, 0), (2, 0)], qtok, counts, None
-    )
-    store_x, own = lax.optimization_barrier((store_x, own))
+    near = {0: store, 2: store_c}
+    result = score(where, line[:2], 0, near, counts, qtok, None)
+    result = score(where, line[2:], 2, near, counts, qtok, result)
+    store_x, result = lax.optimization_barrier((store_x, result))
     store_xc = move(store_x, lambda yh, c, zh, x: (yh, 1 - c, zh, x))
+    result = score(where, beside, z_count, near, counts, qtok, result)
     everything = score(
-        where,
-        blocks,
-        at,
-        [passages, store_c, store_x, store_xc],
-        [(0, z_count), (2, z_count), (1, 0), (3, 0)],
-        qtok,
-        counts,
-        own,
+        where, line + beside, 0, {1: store_x, 3: store_xc}, counts, qtok, result
     )
     returned = everything.reshape(cells, query_count, SETS * slots)
     members = [

time: 72 us -> 71 us (0.986)
  local copies, waits for them, and re-layouts: 2.13 us -> 0 us
  blocking collectives: 12.9 us -> 15 us
  waiting for transfers between devices: 21.9 us -> 20.5 us
  Pallas kernels: 23 us -> 24 us
    unnamed x4 -> x0, local copies, waits for them, and re-layouts: 2.13 us -> none
    all_to_all x1, blocking collectives: 12.9 us -> 15 us  [local(): lax.all_to_all(returned, AXES, 0, 0, tiled=True, axis_index_groups=members)]
    pallas_call x2 -> x4, Pallas kernels: 19.5 us -> 21 us  [score(): pl.pallas_call(functools.partial(score_kernel, plan), out_shape=jax.Shape...]
    ppermute x10, waiting for transfers between devices: 21.9 us -> 20.5 us  [move(): return lax.ppermute(value, AXES, pairs)]
    pallas_call x1, Pallas kernels: 1.69 us -> 0.79 us  [select(): pl.pallas_call(select_kernel, out_shape=jax.ShapeDtypeStruct((pick.shape[...]
  transfers between devices with their start and end apart: 10 -> 10, of which waited for: 6 -> 8; matrix products, arithmetic and copies ran while one was open for 0% -> 0% of each run, Pallas kernels for 13% -> 24%
where the time goes in v1:
time: 71 us; the launch traced here: 70.8 us
  Pallas kernels  24 us (34%)
  waiting for transfers between devices  20.5 us (29%)
  blocking collectives  15 us (21%)
  starting transfers between devices  11.3 us (16%)
    pallas_call x4, Pallas kernels, score(): pl.pallas_call(functools.partial(score_kernel, plan), out_shape=jax.Shape...  21 us
    ppermute x10, waiting for transfers between devices, move(): return lax.ppermute(value, AXES, pairs)  20.5 us
    all_to_all x1, blocking collectives, local(): lax.all_to_all(returned, AXES, 0, 0, tiled=True, axis_index_groups=members)  15 us
    ppermute x10, starting transfers between devices, move(): return lax.ppermute(value, AXES, pairs)  11.3 us
    pallas_call x1, Pallas kernels, prepare(): pl.pallas_call(functools.partial(prepare_kernel, shape), out_shape=(jax.S...  2.16 us
  transfers between devices with their start and end apart: 10, of which 8 were waited for; matrix products, arithmetic and copies ran while one was open for 0% of the time, Pallas kernels for 24%

profile of v1, /device:TPU:0, one launch (start us, length us, event | category | flops | bytes accessed | tf_op | source)
XLA Modules:
  0.0 70.8 jit_solution(5803395231192491615)
XLA Ops:
  0.0 0.5 collective-permute-start.8
  0.5 2.5 %collective-permute-start.7 = (bf16[64,64,128]{2,1,0:T(8,128)(2,1)}, bf16[64,64,128]{2,1,0:T(8,128)(2,1)S(1)}, u32[]{:S(2)}, u32[]{:S(2)}) collective-permute-start(bf16[64,64,128]{2,1,0:T(8,128)(2,1)} %store_ref.1), channel_id=1, source_target_pairs={{0,1},{1,0},{2,3},{3,2},{4,5},{5,4},{6,7},{7,6},{8,9},{9,8},{10,11... | collective-permute-start | bytes 3145736 | tf_op jit(solution)/shard_map/ppermute | solution.py:350
  3.0 2.2 %prepare.1 = (bf16[528,128]{1,0:T(8,128)(2,1)S(1)}, s32[16,256]{1,0:T(8,128)S(1)}, bf16[64,64,128]{2,1,0:T(8,128)(2,1)S(1)}) custom-call(s32[1]{0:T(128)} %bitcast.where_ref.refs_0_, bf16[16,32,128]{2,1,0:T(8,128)(2,1)} %query_ref.1, s32[16,160]{1,0:T(8,128)} %cand_ref.1, s32[16,128]{1,0:T(8,128)} %bitcast.4, bf16[64,64,128]{2,1,0:T(8,128)(2,1)} %store_ref.1), custom_call_target="tpu_custom_call" | custom-call | tf_op jit(solution)/shard_map/prepare/pallas_call | solution.py:75
  5.1 1.6 %collective-permute-start = (bf16[528,128]{1,0:T(8,128)(2,1)S(1)}, bf16[528,128]{1,0:T(8,128)(2,1)S(1)}, u32[]{:S(2)}, u32[]{:S(2)}) collective-permute-start(bf16[528,128]{1,0:T(8,128)(2,1)S(1)} %get-tuple-element.10.refs_1_), channel_id=1, source_target_pairs={{0,2},{1,3},{2,0},{3,1},{4,6},{5,7},{6,4},{7,5},{8,10},{9,11},{10,... | collective-permute-start | bytes 405512 | tf_op jit(solution)/shard_map/ppermute | solution.py:350
  6.8 2.5 %collective-permute-start.2 = (bf16[528,128]{1,0:T(8,128)(2,1)S(1)}, bf16[528,128]{1,0:T(8,128)(2,1)S(1)}, u32[]{:S(2)}, u32[]{:S(2)}) collective-permute-start(bf16[528,128]{1,0:T(8,128)(2,1)S(1)} %get-tuple-element.10.refs_1_), channel_id=1, source_target_pairs={{0,6},{1,7},{2,4},{3,5},{4,2},{5,3},{6,0},{7,1},{8,14},{9,15},{10,... | collective-permute-start | bytes 405512 | tf_op jit(solution)/shard_map/ppermute | solution.py:350
  9.3 0.1 collective-permute-start.1
  9.4 1.5 %collective-permute-done.refs_2_ = bf16[528,128]{1,0:T(8,128)(2,1)S(1)} collective-permute-done((bf16[528,128]{1,0:T(8,128)(2,1)S(1)}, bf16[528,128]{1,0:T(8,128)(2,1)S(1)}, u32[]{:S(2)}, u32[]{:S(2)}) %collective-permute-start) | collective-permute-done | bytes 135200 | tf_op jit(solution)/shard_map/ppermute | solution.py:350
  10.9 0.0 collective-permute-done.8.refs_4_.refs_6_
  10.9 3.6 %shard_map.46.refs_5_ = f32[128,256]{1,0:T(8,128)S(1)} custom-call(s32[1]{0:T(128)} %bitcast.where_ref.refs_0_, bf16[528,128]{1,0:T(8,128)(2,1)S(1)} %get-tuple-element.10.refs_1_, bf16[528,128]{1,0:T(8,128)(2,1)S(1)} %collective-permute-done.refs_2_, bf16[64,64,128]{2,1,0:T(8,128)(2,1)S(1)} %get-tuple-element.11.refs_3_.refs_5_, ...), custom_call_target="tpu_custom_call" | custom-call | flops 1073741824 | bytes 2367488 | tf_op jit(solution)/shard_map/pallas_call | solution.py:276
  14.5 2.2 %collective-permute-done.2.refs_2_.refs_4_ = bf16[528,128]{1,0:T(8,128)(2,1)S(1)} collective-permute-done((bf16[528,128]{1,0:T(8,128)(2,1)S(1)}, bf16[528,128]{1,0:T(8,128)(2,1)S(1)}, u32[]{:S(2)}, u32[]{:S(2)}) %collective-permute-start.2) | collective-permute-done | bytes 135200 | tf_op jit(solution)/shard_map/ppermute | solution.py:350
  16.7 5.1 %collective-permute-done.1.refs_1_.refs_3_ = bf16[528,128]{1,0:T(8,128)(2,1)S(1)} collective-permute-done((bf16[528,128]{1,0:T(8,128)(2,1)S(1)}, bf16[528,128]{1,0:T(8,128)(2,1)S(1)}, u32[]{:S(2)}, u32[]{:S(2)}) %collective-permute-start.1) | collective-permute-done | bytes 135200 | tf_op jit(solution)/shard_map/ppermute | solution.py:350
  21.8 4.3 %shard_map.47.refs_7_ = f32[128,256]{1,0:T(8,128)S(1)} custom-call(s32[1]{0:T(128)} %bitcast.where_ref.refs_0_, bf16[528,128]{1,0:T(8,128)(2,1)S(1)} %collective-permute-done.1.refs_1_.refs_3_, bf16[528,128]{1,0:T(8,128)(2,1)S(1)} %collective-permute-done.2.refs_2_.refs_4_, bf16[64,64,128]{2,1,0:T(8,128)(2,1)S(1)} %get-tuple-element.11.refs_3_.refs_5_, ...), custom_call_target="tpu_custom_call" | custom-call | flops 1073741824 | bytes 2367488 | tf_op jit(solution)/shard_map/pallas_call | solution.py:276
  26.0 1.0 %collective-permute-done.7.refs_9_ = bf16[64,64,128]{2,1,0:T(8,128)(2,1)S(1)} collective-permute-done((bf16[64,64,128]{2,1,0:T(8,128)(2,1)}, bf16[64,64,128]{2,1,0:T(8,128)(2,1)S(1)}, u32[]{:S(2)}, u32[]{:S(2)}) %collective-permute-start.7) | collective-permute-done | bytes 1048608 | tf_op jit(solution)/shard_map/ppermute | solution.py:350
  27.0 0.0 collective-permute-start.9
  27.0 1.8 %collective-permute-start.3 = (bf16[528,128]{1,0:T(8,128)(2,1)S(1)}, bf16[528,128]{1,0:T(8,128)(2,1)S(1)}, u32[]{:S(2)}, u32[]{:S(2)}) collective-permute-start(bf16[528,128]{1,0:T(8,128)(2,1)S(1)} %get-tuple-element.10.refs_1_), channel_id=1, source_target_pairs={{0,16},{1,17},{2,18},{3,19},{4,20},{5,21},{6,22},{7,23},{8,24},{9,... | collective-permute-start | bytes 405512 | tf_op jit(solution)/shard_map/ppermute | solution.py:350
  28.8 0.3 collective-permute-start.6
  29.0 1.8 %collective-permute-start.5 = (bf16[528,128]{1,0:T(8,128)(2,1)S(1)}, bf16[528,128]{1,0:T(8,128)(2,1)S(1)}, u32[]{:S(2)}, u32[]{:S(2)}) collective-permute-start(bf16[528,128]{1,0:T(8,128)(2,1)S(1)} %collective-permute-done.1.refs_1_.refs_3_), channel_id=1, source_target_pairs={{0,16},{1,17},{2,18},{3,19},{4,20},{5,21},{6,22},{7,23},{8,24},{9,... | collective-permute-start | bytes 405512 | tf_op jit(solution)/shard_map/ppermute | solution.py:350
  30.8 0.3 collective-permute-start.4
  31.1 2.4 %collective-permute-done.3.refs_1_.refs_5_ = bf16[528,128]{1,0:T(8,128)(2,1)S(1)} collective-permute-done((bf16[528,128]{1,0:T(8,128)(2,1)S(1)}, bf16[528,128]{1,0:T(8,128)(2,1)S(1)}, u32[]{:S(2)}, u32[]{:S(2)}) %collective-permute-start.3) | collective-permute-done | bytes 135200 | tf_op jit(solution)/shard_map/ppermute | solution.py:350
  33.5 2.9 %collective-permute-done.6.refs_4_.refs_8_ = bf16[528,128]{1,0:T(8,128)(2,1)S(1)} collective-permute-done((bf16[528,128]{1,0:T(8,128)(2,1)S(1)}, bf16[528,128]{1,0:T(8,128)(2,1)S(1)}, u32[]{:S(2)}, u32[]{:S(2)}) %collective-permute-start.6) | collective-permute-done | bytes 135200 | tf_op jit(solution)/shard_map/ppermute | solution.py:350
  36.4 2.9 %collective-permute-done.5.refs_3_.refs_7_ = bf16[528,128]{1,0:T(8,128)(2,1)S(1)} collective-permute-done((bf16[528,128]{1,0:T(8,128)(2,1)S(1)}, bf16[528,128]{1,0:T(8,128)(2,1)S(1)}, u32[]{:S(2)}, u32[]{:S(2)}) %collective-permute-start.5) | collective-permute-done | bytes 135200 | tf_op jit(solution)/shard_map/ppermute | solution.py:350
  39.3 2.5 %collective-permute-done.4.refs_2_.refs_6_ = bf16[528,128]{1,0:T(8,128)(2,1)S(1)} collective-permute-done((bf16[528,128]{1,0:T(8,128)(2,1)S(1)}, bf16[528,128]{1,0:T(8,128)(2,1)S(1)}, u32[]{:S(2)}, u32[]{:S(2)}) %collective-permute-start.4) | collective-permute-done | bytes 135200 | tf_op jit(solution)/shard_map/ppermute | solution.py:350
  41.7 6.9 %shard_map.48.refs_11_ = f32[128,256]{1,0:T(8,128)S(1)} custom-call(s32[1]{0:T(128)} %bitcast.where_ref.refs_0_, bf16[528,128]{1,0:T(8,128)(2,1)S(1)} %collective-permute-done.3.refs_1_.refs_5_, bf16[528,128]{1,0:T(8,128)(2,1)S(1)} %collective-permute-done.4.refs_2_.refs_6_, bf16[528,128]{1,0:T(8,128)(2,1)S(1)} %collective-permute-done.5.refs_3_.refs_7_, ...), custom_call_target="tpu_custom_call" | custom-call | flops 2147483648 | bytes 2637824 | tf_op jit(solution)/shard_map/pallas_call | solution.py:276
  48.6 0.0 collective-permute-done.9.refs_10_
  48.6 6.3 %shard_map.49 = f32[128,256]{1,0:T(8,128)S(1)} custom-call(s32[1]{0:T(128)} %bitcast.where_ref.refs_0_, bf16[528,128]{1,0:T(8,128)(2,1)S(1)} %get-tuple-element.10.refs_1_, bf16[528,128]{1,0:T(8,128)(2,1)S(1)} %collective-permute-done.refs_2_, bf16[528,128]{1,0:T(8,128)(2,1)S(1)} %collective-permute-done.1.refs_1_.refs_3_, ...), custom_call_target="tpu_custom_call" | custom-call | flops 4294967296 | bytes 3178496 | tf_op jit(solution)/shard_map/pallas_call | solution.py:276
  55.0 15.0 %all_to_all.5.scores_ref = f32[8,16,256]{2,1,0:T(8,128)S(1)} all-to-all(f32[8,16,256]{2,1,0:T(8,128)S(1)} %bitcast.3), channel_id=1, replica_groups={{0,2,4,6,16,18,20,22},{1,3,5,7,17,19,21,23},{8,10,12,14,24,26,28,30},{9..., dimensions={0} | all-to-all | bytes 262144 | tf_op jit(solution)/shard_map/all_to_all | solution.py:389
  70.0 0.8 %select.1 = f32[16,160]{1,0:T(8,128)} custom-call(f32[8,16,256]{2,1,0:T(8,128)S(1)} %all_to_all.5.scores_ref, s32[16,256]{1,0:T(8,128)S(1)} %get-tuple-element.14.pick_ref), custom_call_target="tpu_custom_call" | custom-call | tf_op jit(solution)/shard_map/select/pallas_call | solution.py:319
Async XLA Ops:
  0.0 10.9 %collective-permute-start.8 = (bf16[64,64,128]{2,1,0:T(8,128)(2,1)}, bf16[64,64,128]{2,1,0:T(8,128)(2,1)S(1)}, u32[]{:S(2)}, u32[]{:S(2)}) collective-permute-start(bf16[64,64,128]{2,1,0:T(8,128)(2,1)} %store_ref.1), channel_id=1, source_target_pairs={{0,8},{1,9},{2,10},{3,11},{4,12},{5,13},{6,14},{7,15},{8,0},{9,1},... | collective-permute-start | bytes 3145736 | tf_op jit(solution)/shard_map/ppermute | solution.py:350
  0.5 26.5 %collective-permute-start.7 = (bf16[64,64,128]{2,1,0:T(8,128)(2,1)}, bf16[64,64,128]{2,1,0:T(8,128)(2,1)S(1)}, u32[]{:S(2)}, u32[]{:S(2)}) collective-permute-start(bf16[64,64,128]{2,1,0:T(8,128)(2,1)} %store_ref.1), channel_id=1, source_target_pairs={{0,1},{1,0},{2,3},{3,2},{4,5},{5,4},{6,7},{7,6},{8,9},{9,8},{10,11... | collective-permute-start | bytes 3145736 | tf_op jit(solution)/shard_map/ppermute | solution.py:350
  5.1 5.8 %collective-permute-start = (bf16[528,128]{1,0:T(8,128)(2,1)S(1)}, bf16[528,128]{1,0:T(8,128)(2,1)S(1)}, u32[]{:S(2)}, u32[]{:S(2)}) collective-permute-start(bf16[528,128]{1,0:T(8,128)(2,1)S(1)} %get-tuple-element.10.refs_1_), channel_id=1, source_target_pairs={{0,2},{1,3},{2,0},{3,1},{4,6},{5,7},{6,4},{7,5},{8,10},{9,11},{10,... | collective-permute-start | bytes 405512 | tf_op jit(solution)/shard_map/ppermute | solution.py:350
  6.8 9.9 %collective-permute-start.2 = (bf16[528,128]{1,0:T(8,128)(2,1)S(1)}, bf16[528,128]{1,0:T(8,128)(2,1)S(1)}, u32[]{:S(2)}, u32[]{:S(2)}) collective-permute-start(bf16[528,128]{1,0:T(8,128)(2,1)S(1)} %get-tuple-element.10.refs_1_), channel_id=1, source_target_pairs={{0,6},{1,7},{2,4},{3,5},{4,2},{5,3},{6,0},{7,1},{8,14},{9,15},{10,... | collective-permute-start | bytes 405512 | tf_op jit(solution)/shard_map/ppermute | solution.py:350
  9.3 12.5 %collective-permute-start.1 = (bf16[528,128]{1,0:T(8,128)(2,1)S(1)}, bf16[528,128]{1,0:T(8,128)(2,1)S(1)}, u32[]{:S(2)}, u32[]{:S(2)}) collective-permute-start(bf16[528,128]{1,0:T(8,128)(2,1)S(1)} %get-tuple-element.10.refs_1_), channel_id=1, source_target_pairs={{0,4},{1,5},{2,6},{3,7},{4,0},{5,1},{6,2},{7,3},{8,12},{9,13},{10,... | collective-permute-start | bytes 405512 | tf_op jit(solution)/shard_map/ppermute | solution.py:350
  27.0 21.6 %collective-permute-start.9 = (bf16[64,64,128]{2,1,0:T(8,128)(2,1)S(1)}, bf16[64,64,128]{2,1,0:T(8,128)(2,1)S(1)}, u32[]{:S(2)}, u32[]{:S(2)}) collective-permute-start(bf16[64,64,128]{2,1,0:T(8,128)(2,1)S(1)} %collective-permute-done.7.refs_9_), channel_id=1, source_target_pairs={{0,8},{1,9},{2,10},{3,11},{4,12},{5,13},{6,14},{7,15},{8,0},{9,1},... | collective-permute-start | bytes 3145736 | tf_op jit(solution)/shard_map/ppermute | solution.py:350
  27.0 6.5 %collective-permute-start.3 = (bf16[528,128]{1,0:T(8,128)(2,1)S(1)}, bf16[528,128]{1,0:T(8,128)(2,1)S(1)}, u32[]{:S(2)}, u32[]{:S(2)}) collective-permute-start(bf16[528,128]{1,0:T(8,128)(2,1)S(1)} %get-tuple-element.10.refs_1_), channel_id=1, source_target_pairs={{0,16},{1,17},{2,18},{3,19},{4,20},{5,21},{6,22},{7,23},{8,24},{9,... | collective-permute-start | bytes 405512 | tf_op jit(solution)/shard_map/ppermute | solution.py:350
  28.8 7.6 %collective-permute-start.6 = (bf16[528,128]{1,0:T(8,128)(2,1)S(1)}, bf16[528,128]{1,0:T(8,128)(2,1)S(1)}, u32[]{:S(2)}, u32[]{:S(2)}) collective-permute-start(bf16[528,128]{1,0:T(8,128)(2,1)S(1)} %collective-permute-done.2.refs_2_.refs_4_), channel_id=1, source_target_pairs={{0,16},{1,17},{2,18},{3,19},{4,20},{5,21},{6,22},{7,23},{8,24},{9,... | collective-permute-start | bytes 405512 | tf_op jit(solution)/shard_map/ppermute | solution.py:350
  29.0 10.2 %collective-permute-start.5 = (bf16[528,128]{1,0:T(8,128)(2,1)S(1)}, bf16[528,128]{1,0:T(8,128)(2,1)S(1)}, u32[]{:S(2)}, u32[]{:S(2)}) collective-permute-start(bf16[528,128]{1,0:T(8,128)(2,1)S(1)} %collective-permute-done.1.refs_1_.refs_3_), channel_id=1, source_target_pairs={{0,16},{1,17},{2,18},{3,19},{4,20},{5,21},{6,22},{7,23},{8,24},{9,... | collective-permute-start | bytes 405512 | tf_op jit(solution)/shard_map/ppermute | solution.py:350
  30.8 10.9 %collective-permute-start.4 = (bf16[528,128]{1,0:T(8,128)(2,1)S(1)}, bf16[528,128]{1,0:T(8,128)(2,1)S(1)}, u32[]{:S(2)}, u32[]{:S(2)}) collective-permute-start(bf16[528,128]{1,0:T(8,128)(2,1)S(1)} %collective-permute-done.refs_2_), channel_id=1, source_target_pairs={{0,16},{1,17},{2,18},{3,19},{4,20},{5,21},{6,22},{7,23},{8,24},{9,... | collective-permute-start | bytes 405512 | tf_op jit(solution)/shard_map/ppermute | solution.py:350
